TPU v7x, 32 devices: a whole 2x2x4 slice. The times are simulated.
32 devices in a mesh: replica: 2 (over y), shard: 2 (over x), tensor: 8 (over z, core).
Axes of the slice: x: 2, y: 2, z: 4, core: 2. Of those that a mesh axis runs over, the one named last changes fastest.
Arguments:
- layer_input: bfloat16 [32768, 1024], P(('replica', 'shard', 'tensor')), may hold values from -6 to 6
- segment_ids: int32 [32, 1024], P(('replica', 'shard')), may hold values from 0 to 3, as said below
- qkv_weight: bfloat16 [3, 1024, 1024], P(None, 'shard', 'tensor'), may hold values from -0.1875 to 0.1875
- qkv_bias: float32 [2, 1024], P(None, 'tensor'), may hold values from -1.2 to 1.2
- out_weight: bfloat16 [1024, 1024], P('tensor', 'shard'), may hold values from -1.5 to 1.5
- out_bias: float32 [1024], replicated, may hold values from -3 to 3
- norm1_gain: float32 [1024], replicated, may hold values from 0.5 to 1.5
- norm1_bias: float32 [1024], replicated, may hold values from -3 to 3
- up_weight: bfloat16 [1024, 4096], P('shard', 'tensor'), may hold values from -0.1875 to 0.1875
- up_bias: float32 [4096], P('tensor'), may hold values from -3 to 3
- down_weight: bfloat16 [4096, 1024], P('tensor', 'shard'), may hold values from -0.09375 to 0.09375
- down_bias: float32 [1024], replicated, may hold values from -3 to 3
- norm2_gain: float32 [1024], replicated, may hold values from 0.5 to 1.5
- norm2_bias: float32 [1024], replicated, may hold values from -3 to 3
- output_grad: bfloat16 [32768, 1024], P(('replica', 'shard', 'tensor')), may hold values from -6 to 6
Outputs:
- activations: bfloat16 [32768, 1024], P(('replica', 'shard', 'tensor'))
- input_grad: float32 [32768, 1024], P(('replica', 'shard', 'tensor'))
- qkv_weight_grad: float32 [3, 1024, 1024], P(None, 'shard', 'tensor')
- qkv_bias_grad: float32 [2, 1024], P(None, 'tensor')
- out_weight_grad: float32 [1024, 1024], P('tensor', 'shard')
- out_bias_grad: float32 [1024], replicated
- norm1_gain_grad: float32 [1024], replicated
- norm1_bias_grad: float32 [1024], replicated
- up_weight_grad: float32 [1024, 4096], P('shard', 'tensor')
- up_bias_grad: float32 [4096], P('tensor')
- down_weight_grad: float32 [4096, 1024], P('tensor', 'shard')
- down_bias_grad: float32 [1024], replicated
- norm2_gain_grad: float32 [1024], replicated
- norm2_bias_grad: float32 [1024], replicated
Inputs may be any that keep to these rules, and one draw needn't show every extreme that they name: `segment_ids`: within each sequence the ids never fall and every id from 0 to 3 occurs; each document holds 128 to 512 tokens, and one in each sequence holds exactly 512.
All inputs are finite; a program needn't handle non-finite values.
Results may differ from a plain program's by a relative error of at most 0.02.
Values may be sent and summed in bfloat16 or wider, within the bound.
No kernel may reach another device: no remote copies, remote signals or barrier semaphores. Data moves between devices by JAX's collectives and lax.ppermute only.
A program may use at most 256 MiB of HBM per device.

v0:
```python
import math
import jax
import jax.numpy as jnp
from jax import lax
from jax.sharding import PartitionSpec as P

HEAD_DIM = 64
LEN = 1024
EPSILON = 1e-05
NEG_FILL = -1e30
CONTRACT_ROWS = (((0,), (0,)), ((), ()))
CONTRACT_COLS = (((1,), (1,)), ((), ()))
OWNERS = ("shard", "tensor")
EVERYONE = ("replica", "shard", "tensor")


def gather_blocks(weight):
    blocks = lax.all_gather(weight, OWNERS, axis=0, tiled=False)
    return blocks.reshape((lax.axis_size("shard"), lax.axis_size("tensor")) + weight.shape)


def gather_qkv(weight):
    blocks = gather_blocks(weight)
    return blocks.transpose(2, 0, 3, 1, 4).reshape(3, -1, blocks.shape[1] * blocks.shape[4])


def gather_row_col(weight):
    blocks = gather_blocks(weight)
    return blocks.transpose(0, 2, 1, 3).reshape(-1, blocks.shape[1] * blocks.shape[3])


def gather_col_row(weight):
    blocks = gather_blocks(weight)
    return blocks.transpose(1, 2, 0, 3).reshape(-1, blocks.shape[0] * blocks.shape[3])


def scatter_blocks(blocks):
    flat = blocks.reshape((-1,) + blocks.shape[2:])
    owned = lax.psum_scatter(flat, OWNERS, scatter_dimension=0, tiled=False)
    return lax.psum(owned, "replica").astype(jnp.float32)


def scatter_qkv(grad):
    shards, tensors = (lax.axis_size("shard"), lax.axis_size("tensor"))
    three, rows, cols = grad.shape
    blocks = grad.reshape(three, shards, rows // shards, tensors, cols // tensors)
    return scatter_blocks(blocks.transpose(1, 3, 0, 2, 4))


def scatter_row_col(grad):
    shards, tensors = (lax.axis_size("shard"), lax.axis_size("tensor"))
    rows, cols = grad.shape
    blocks = grad.reshape(shards, rows // shards, tensors, cols // tensors)
    return scatter_blocks(blocks.transpose(0, 2, 1, 3))


def scatter_col_row(grad):
    shards, tensors = (lax.axis_size("shard"), lax.axis_size("tensor"))
    rows, cols = grad.shape
    blocks = grad.reshape(tensors, rows // tensors, shards, cols // shards)
    return scatter_blocks(blocks.transpose(2, 0, 1, 3))


def normalize(residual, gain_vec, shift_vec):
    center = residual - jnp.mean(residual, axis=-1, keepdims=True)
    spread = lax.rsqrt(jnp.mean(center * center, axis=-1, keepdims=True) + EPSILON)
    normed = center * spread
    return (normed * gain_vec + shift_vec, normed, spread)


def norm_back(incoming, normed, spread, gain_vec):
    scaled = incoming * gain_vec
    back_grad = spread * (
        scaled
        - jnp.mean(scaled, axis=-1, keepdims=True)
        - normed * jnp.mean(scaled * normed, axis=-1, keepdims=True)
    )
    return (back_grad, jnp.sum(incoming * normed, axis=0), jnp.sum(incoming, axis=0))


def masked_scores(queries, key_rows, same_doc):
    scores = jnp.einsum(
        "qhd,khd->hqk", queries, key_rows, preferred_element_type=jnp.float32
    ) * HEAD_DIM ** (-0.5)
    return jnp.where(same_doc[None], scores, NEG_FILL)


def attend(queries, key_rows, value_rows, same_doc):
    scores = masked_scores(queries, key_rows, same_doc)
    row_max = jnp.max(scores, axis=-1, keepdims=True)
    raw_weights = jnp.exp(scores - row_max)
    row_total = jnp.sum(raw_weights, axis=-1, keepdims=True)
    attn_probs = raw_weights / row_total
    log_total = row_max + jnp.log(row_total)
    mixed_heads = jnp.einsum(
        "hqk,khd->qhd",
        attn_probs.astype(jnp.bfloat16),
        value_rows,
        preferred_element_type=jnp.float32,
    )
    return (mixed_heads.astype(jnp.bfloat16), log_total)


def attend_back(queries, key_rows, value_rows, same_doc, log_total, mixed_grad):
    scores = masked_scores(queries, key_rows, same_doc)
    attn_probs = jnp.exp(scores - log_total)
    prob_grad = jnp.einsum(
        "qhd,khd->hqk", mixed_grad, value_rows, preferred_element_type=jnp.float32
    )
    value_grad = jnp.einsum(
        "hqk,qhd->khd",
        attn_probs.astype(jnp.bfloat16),
        mixed_grad,
        preferred_element_type=jnp.float32,
    )
    inner_sum = jnp.sum(attn_probs * prob_grad, axis=-1, keepdims=True)
    score_low = (attn_probs * (prob_grad - inner_sum)).astype(jnp.bfloat16)
    query_grad = jnp.einsum(
        "hqk,khd->qhd", score_low, key_rows, preferred_element_type=jnp.float32
    ) * HEAD_DIM ** (-0.5)
    key_grad = jnp.einsum(
        "hqk,qhd->khd", score_low, queries, preferred_element_type=jnp.float32
    ) * HEAD_DIM ** (-0.5)
    return (query_grad, key_grad, value_grad)


def body(
    layer_input,
    segment_ids,
    qkv_weight,
    qkv_bias,
    out_weight,
    out_bias,
    norm1_gain,
    norm1_bias,
    up_weight,
    up_bias,
    down_weight,
    down_bias,
    norm2_gain,
    norm2_bias,
    output_grad,
):
    rows, width = layer_input.shape
    tensor_index = lax.axis_index("tensor")
    tensor_count = lax.axis_size("tensor")
    sharers = max(1, LEN // rows)
    seqs_here = max(1, rows // LEN)
    query_rows = min(rows, LEN)
    sharing = [list(range(i, i + sharers)) for i in range(0, tensor_count, sharers)]
    w_qkv = gather_qkv(qkv_weight)
    bias_qkv = lax.all_gather(qkv_bias, "tensor", axis=1, tiled=True)
    bias_up = lax.all_gather(up_bias, "tensor", axis=0, tiled=True)
    w_out = gather_col_row(out_weight)
    w_up = gather_row_col(up_weight)
    w_down = gather_col_row(down_weight)
    first_seq = tensor_index * rows // LEN
    key_segments = lax.dynamic_slice_in_dim(segment_ids, first_seq, seqs_here, 0)
    query_start = tensor_index * rows % LEN
    query_segments = lax.dynamic_slice_in_dim(key_segments, query_start, query_rows, 1)
    same_doc = query_segments[:, :, None] == key_segments[:, None, :]
    heads = width // HEAD_DIM
    group = 2

    def by_head(rows_array, length):
        split = rows_array.reshape(seqs_here, length, heads // group, group, HEAD_DIM)
        return split.transpose(0, 2, 1, 3, 4)

    def from_heads(blocks):
        return blocks.transpose(0, 2, 1, 3, 4).reshape(-1, width)

    def whole_rows(rows_array):
        if sharers == 1:
            return rows_array
        return lax.all_gather(rows_array, "tensor", axis_index_groups=sharing, axis=0, tiled=True)

    def own_rows(rows_array):
        if sharers == 1:
            return rows_array
        return lax.psum_scatter(
            rows_array, "tensor", axis_index_groups=sharing, scatter_dimension=0, tiled=True
        )

    projected = jnp.einsum("td,jdc->jtc", layer_input, w_qkv, preferred_element_type=jnp.float32)
    queries = (projected[0] + bias_qkv[0]).astype(jnp.bfloat16)
    key_rows = whole_rows(projected[1].astype(jnp.bfloat16))
    value_rows = whole_rows((projected[2] + bias_qkv[1]).astype(jnp.bfloat16))
    queries = by_head(queries, query_rows)
    key_rows = by_head(key_rows, LEN)
    value_rows = by_head(value_rows, LEN)
    mixed, log_total = ([], [])
    for s in range(seqs_here):
        one_mixed, one_log = lax.map(
            lambda item: attend(*item, same_doc[s]), (queries[s], key_rows[s], value_rows[s])
        )
        mixed.append(one_mixed)
        log_total.append(one_log)
    mixed_rows = from_heads(jnp.stack(mixed))
    residual_one = (
        layer_input.astype(jnp.float32)
        + jnp.dot(mixed_rows, w_out, preferred_element_type=jnp.float32)
        + out_bias
    )
    hidden_one, normed_one, spread_one = normalize(residual_one, norm1_gain, norm1_bias)
    hidden_low = hidden_one.astype(jnp.bfloat16)
    pre_act = jnp.dot(hidden_low, w_up, preferred_element_type=jnp.float32) + bias_up
    activ = jax.nn.gelu(pre_act, approximate=False).astype(jnp.bfloat16)
    residual_two = (
        hidden_one + jnp.dot(activ, w_down, preferred_element_type=jnp.float32) + down_bias
    )
    final_out, normed_two, spread_two = normalize(residual_two, norm2_gain, norm2_bias)
    resid_two_grad, gain_two_grad, shift_two_grad = norm_back(
        output_grad.astype(jnp.float32), normed_two, spread_two, norm2_gain
    )
    down_bias_part = jnp.sum(resid_two_grad, axis=0)
    branch_grad = resid_two_grad.astype(jnp.bfloat16)
    down_grad = lax.dot_general(
        activ, branch_grad, CONTRACT_ROWS, preferred_element_type=jnp.float32
    ).astype(jnp.bfloat16)
    down_owned = scatter_col_row(down_grad)
    activ_grad = lax.dot_general(
        branch_grad, w_down, CONTRACT_COLS, preferred_element_type=jnp.float32
    )
    normal_cdf = 0.5 * (1.0 + lax.erf(pre_act * (1.0 / math.sqrt(2.0))))
    normal_pdf = jnp.exp(-0.5 * pre_act * pre_act) * (1.0 / math.sqrt(2.0 * math.pi))
    pre_grad = activ_grad * (normal_cdf + pre_act * normal_pdf)
    up_bias_part = jnp.sum(pre_grad, axis=0)
    pre_low = pre_grad.astype(jnp.bfloat16)
    up_grad = lax.dot_general(
        hidden_low, pre_low, CONTRACT_ROWS, preferred_element_type=jnp.float32
    ).astype(jnp.bfloat16)
    up_owned = scatter_row_col(up_grad)
    back_middle = lax.dot_general(pre_low, w_up, CONTRACT_COLS, preferred_element_type=jnp.float32)
    resid_one_grad, gain_one_grad, shift_one_grad = norm_back(
        resid_two_grad + back_middle, normed_one, spread_one, norm1_gain
    )
    out_bias_part = jnp.sum(resid_one_grad, axis=0)
    attn_grad = resid_one_grad.astype(jnp.bfloat16)
    out_grad = lax.dot_general(
        mixed_rows, attn_grad, CONTRACT_ROWS, preferred_element_type=jnp.float32
    ).astype(jnp.bfloat16)
    out_owned = scatter_col_row(out_grad)
    mixed_grad = lax.dot_general(
        attn_grad, w_out, CONTRACT_COLS, preferred_element_type=jnp.float32
    ).astype(jnp.bfloat16)
    mixed_grad = by_head(mixed_grad, query_rows)
    query_grad, key_grad, value_grad = ([], [], [])
    for s in range(seqs_here):
        grads = lax.map(
            lambda item: attend_back(item[0], item[1], item[2], same_doc[s], item[3], item[4]),
            (queries[s], key_rows[s], value_rows[s], log_total[s], mixed_grad[s]),
        )
        query_grad.append(grads[0])
        key_grad.append(grads[1])
        value_grad.append(grads[2])
    query_grad = from_heads(jnp.stack(query_grad))
    key_grad = own_rows(from_heads(jnp.stack(key_grad)))
    value_grad = own_rows(from_heads(jnp.stack(value_grad)))
    proj_low = [grad.astype(jnp.bfloat16) for grad in (query_grad, key_grad, value_grad)]
    qkv_grad = jnp.stack(
        [
            lax.dot_general(
                layer_input, grad, CONTRACT_ROWS, preferred_element_type=jnp.float32
            ).astype(jnp.bfloat16)
            for grad in proj_low
        ]
    )
    qkv_owned = scatter_qkv(qkv_grad)
    input_grad = resid_one_grad
    for j in range(3):
        input_grad = input_grad + lax.dot_general(
            proj_low[j], w_qkv[j], CONTRACT_COLS, preferred_element_type=jnp.float32
        )
    parts = (
        jnp.sum(query_grad, axis=0),
        jnp.sum(value_grad, axis=0),
        up_bias_part,
        out_bias_part,
        gain_one_grad,
        shift_one_grad,
        down_bias_part,
        gain_two_grad,
        shift_two_grad,
    )
    summed = jnp.sum(lax.all_gather(jnp.concatenate(parts), EVERYONE, axis=0, tiled=False), axis=0)
    ends = [0]
    for part in parts:
        ends.append(ends[-1] + part.shape[0])
    summed = [summed[ends[i] : ends[i + 1]] for i in range(len(parts))]
    width_here = qkv_bias.shape[1]
    hidden_here = up_bias.shape[0]
    qkv_bias_grad = lax.dynamic_slice_in_dim(
        jnp.stack(summed[:2]), tensor_index * width_here, width_here, 1
    )
    up_bias_grad = lax.dynamic_slice_in_dim(summed[2], tensor_index * hidden_here, hidden_here, 0)
    return (
        final_out.astype(jnp.bfloat16),
        input_grad,
        qkv_owned,
        qkv_bias_grad,
        out_owned,
        summed[3],
        summed[4],
        summed[5],
        up_owned,
        up_bias_grad,
        down_owned,
        summed[6],
        summed[7],
        summed[8],
    )


def solution(mesh):
    placed = (
        P(("replica", "shard", "tensor"), None),
        P(("replica", "shard"), None),
        P(None, "shard", "tensor"),
        P(None, "tensor"),
        P("tensor", "shard"),
        P(),
        P(),
        P(),
        P("shard", "tensor"),
        P("tensor"),
        P("tensor", "shard"),
        P(),
        P(),
        P(),
        P(("replica", "shard", "tensor"), None),
    )
    return jax.shard_map(
        body,
        mesh=mesh,
        in_specs=placed,
        out_specs=(
            P(("replica", "shard", "tensor"), None),
            P(("replica", "shard", "tensor"), None),
            P(None, "shard", "tensor"),
            P(None, "tensor"),
            P("tensor", "shard"),
            P(),
            P(),
            P(),
            P("shard", "tensor"),
            P("tensor"),
            P("tensor", "shard"),
            P(),
            P(),
            P(),
        ),
        check_vma=False,
    )
```

profile of v0, /device:TPU:0, one launch (start us, length us, event | category | flops | bytes accessed | tf_op | source)
XLA Modules:
  0.0 1084.6 jit_solution(9665924579139208757)
XLA Ops:
  10.1 13.7 %all_gather.38 = f32[2,1024]{1,0:T(2,128)S(1)} all-gather(f32[2,128]{1,0:T(2,128)} %param.22), channel_id=1, replica_groups=mesh['replica'=2,'shard'=2,'tensor'=8] {'tensor'}, dimensions={1}, use_global_device_ids=true | all-gather | bytes 9216 | tf_op jit(solution)/shard_map/all_gather | solution.py:152
  28.0 12.8 %all-gather.5 = f32[8,1,512]{2,1,0:T(1,128)S(1)} all-gather(f32[1,1,512]{2,1,0:T(1,128)S(1)} %bitcast.312), channel_id=1, replica_groups=mesh['replica'=2,'shard'=2,'tensor'=8] {'tensor'}, dimensions={0}, use_global_device_ids=true | all-gather | bytes 18432 | tf_op jit(solution)/shard_map/all_gather | solution.py:153
  58.8 58.2 %all-gather.12.cloned.1.call-done = bf16[48,512,128]{2,1,0:T(8,128)(2,1)} async-done(((bf16[3,512,128]{2,1,0:T(8,128)(2,1)}), bf16[48,512,128]{2,1,0:T(8,128)(2,1)}) %all-gather.12.cloned.1.call-update) | async-done | bytes 6291472 | tf_op jit(solution)/shard_map/all_gather | solution.py:18
  116.9 16.2 %copy.94 = bf16[2,8,3,512,128]{3,0,4,1,2:T(2,128)(2,1)} copy(bf16[2,8,3,512,128]{4,3,2,1,0:T(8,128)(2,1)} %bitcast.294) | data formatting | bytes 12582912 | tf_op jit(solution)/shard_map/reshape | solution.py:19
  165.1 84.4 %while.28 = (s32[]{:T(128)}, bf16[8,1024,2,64]{1,3,2,0:T(8,128)(2,1)}, f32[8,2,1024,1]{2,1,3,0:T(2,128)}, bf16[8,1024,2,64]{1,3,2,0:T(8,128)(2,1)}, bf16[8,1024,...) while((s32[]{:T(128)}, ...), condition=%wide.region_3.4_spmd.clone, body=%wide.region_0.3_spmd.clone.sunk | while | flops 563214336 | bytes 30480980 | solution.py:193
  258.6 11.5 %copy.96 = bf16[2,8,512,512]{3,1,2,0:T(8,128)(2,1)} copy(bf16[2,8,512,512]{3,2,1,0:T(8,128)(2,1)} %bitcast.279) | data formatting | bytes 16777216 | tf_op jit(solution)/shard_map/reshape | solution.py:19
  270.1 12.6 %copy.120 = bf16[128,8,8,512]{3,1,2,0:T(8,128)(2,1)} copy(bf16[128,8,8,512]{3,2,1,0:T(8,128)(2,1)} %bitcast.269) | data formatting | bytes 16777216
  282.7 14.9 %copy.97 = bf16[2,8,512,512]{2,1,3,0:T(8,128)(2,1)} copy(bf16[2,8,512,512]{3,2,1,0:T(8,128)(2,1)} %bitcast.280) | data formatting | bytes 16777216 | tf_op jit(solution)/shard_map/reshape | solution.py:19
  297.6 12.2 %copy.121 = bf16[128,8,8,512]{3,1,2,0:T(8,128)(2,1)} copy(bf16[128,8,8,512]{3,2,1,0:T(8,128)(2,1)} %bitcast.270) | data formatting | bytes 16777216
  309.9 47.6 %fusion.60 = (bf16[1024,4096]{1,0:T(8,128)(2,1)}, f32[1024,4096]{1,0:T(8,128)}) fusion(f32[4096]{0:T(1024)S(1)} %bitcast.310, bf16[1024,4096]{1,0:T(8,128)(2,1)} %bitcast.281, bf16[1024,1024]{0,1:T(8,128)(2,1)S(1)} %fusion.108.clone.4), kind=kOutput, calls=%fused_computation.67 | convolution fusion | flops 8866758656 | bytes 35667968 | tf_op jit(solution)/shard_map/dot_general | solution.py:206
  357.6 11.6 %fusion.117 = (f32[1024]{0:T(1024)S(1)}, f32[1024,1024]{0,1:T(8,128)S(1)}) fusion(f32[1024]{0:T(1024)S(1)} %copy-done.54, bf16[1024,4096]{1,0:T(8,128)(2,1)} %get-tuple-element.278, bf16[4096,1024]{0,1:T(8,128)(2,1)S(1)} %bitcast.286, f32[1024]{0:T(1024)S(1)} %copy-done.47, f32[1024]{0:T(1024)S(1)} %copy-done.36, f32[1024]{0:T(1024)S(1)} %copy-done.31, ...), kind=kOutput, calls=%fused_computation.176 | convolution fusion | flops 8597273600 | bytes 25190400 | tf_op jit(solution)/shard_map/dot_general | solution.py:209
  373.4 23.7 %fusion.118 = (f32[4096]{0:T(1024)}, bf16[1024,4096]{1,0:T(8,128)(2,1)}) fusion(f32[1024,4096]{1,0:T(8,128)} %get-tuple-element.279, f32[4096]{0:T(1024)S(1)} %bitcast.311, bf16[4096,1024]{0,1:T(8,128)(2,1)} %bitcast.285, f32[1024]{0:T(1024)S(1)} %broadcast_multiply_fusion.2, f32[1024,1024]{0,1:T(8,128)S(1)} %get-tuple-element.281, ...), kind=kOutput, calls=%fused_computation.177 | convolution fusion | flops 8649699328 | bytes 39899136 | tf_op jit(solution)/shard_map/dot_general | solution.py:221
  397.1 15.3 %multiply_reduce_fusion.1 = (f32[1024]{0:T(1024)}, f32[1024]{0:T(1024)S(1)}, f32[1024]{0:T(1024)S(1)}, f32[1024]{0:T(1024)}, f32[1024,1024]{0,1:T(8,128)}) fusion(f32[1024,1024]{0,1:T(8,128)S(1)} %copy-done.3, f32[1024]{0:T(1024)S(1)} %copy-done.31, f32[1024]{0:T(1024)S(1)} %copy-done.25, f32[1024]{0:T(1024)S(1)} %copy-done.36, ...), kind=kOutput, calls=%fused_computation.108 | convolution fusion | flops 8608804864 | bytes 31506432 | tf_op jit(solution)/shard_map/dot_general | solution.py:233
  424.6 154.8 %while.29 = (s32[]{:T(128)}, f32[8,1024,2,64]{1,3,2,0:T(8,128)}, bf16[8,1024,2,64]{1,3,2,0:T(8,128)(2,1)}, f32[8,1024,2,64]{1,3,2,0:T(8,128)}, bf16[8,1024,2,64]...) while((s32[]{:T(128)}, f32[8,1024,2,64]{1,3,2,0:T(8,128)}, ...), condition=%wide.region_14.15_spmd.clone, body=%wide.region_12.14_spmd.clone.sunk | while | flops 1374943232 | bytes 70583408 | solution.py:249
  620.6 12.8 %maximum_bitcast_fusion = bf16[2,8,3,512,128]{3,0,4,1,2:T(2,128)(2,1)} fusion(bf16[1,2,512,8,128]{2,1,4,3,0:T(2,128)(2,1)} %stack.36, bf16[1,2,512,8,128]{2,1,4,3,0:T(2,128)(2,1)} %stack.35, bf16[1,2,512,8,128]{2,1,4,3,0:T(2,128)(2,1)S(1)} %stack.34), kind=kLoop, calls=%fused_computation.91 | loop fusion | flops 6291456 | bytes 12582912 | tf_op jit(solution)/shard_map/transpose | solution.py:47
  633.4 16.2 %copy.104 = bf16[2,8,3,512,128]{4,3,2,1,0:T(8,128)(2,1)} copy(bf16[2,8,3,512,128]{3,0,4,1,2:T(2,128)(2,1)} %maximum_bitcast_fusion) | data formatting | bytes 12582912 | tf_op jit(solution)/shard_map/transpose | solution.py:47
  651.3 16.7 %convolution_convert_fusion = bf16[4096,1024]{1,0:T(8,128)(2,1)} fusion(bf16[1024,4096]{1,0:T(8,128)(2,1)} %get-tuple-element.278, bf16[1024,1024]{0,1:T(8,128)(2,1)S(1)} %copy-done.8, f32[1024,1024]{0,1:T(8,128)} %copy-done.4, f32[1024]{0:T(1024)S(1)} %copy-done.39, f32[1024]{0:T(1024)S(1)} %copy-done.41, f32[1024]{0:T(1024)S(1)} %copy-done.45, ...), kind=kOutput, calls=%fused_computation.89 | convolution fusion | flops 8603566080 | bytes 23089152 | tf_op jit(solution)/shard_map/dot_general | solution.py:217
  668.0 14.9 %reshape.301 = bf16[8,512,2,512]{3,2,1,0:T(2,128)(2,1)} reshape(bf16[4096,1024]{1,0:T(8,128)(2,1)} %convolution_convert_fusion) | data formatting | bytes 16777216 | tf_op jit(solution)/shard_map/reshape | solution.py:60
  692.3 15.5 %convolution_convert_fusion.1 = bf16[1024,4096]{1,0:T(8,128)(2,1)} fusion(bf16[1024,4096]{1,0:T(8,128)(2,1)} %get-tuple-element.284, f32[1024,1024]{0,1:T(8,128)} %copy-done.2, f32[1024]{0:T(1024)S(1)} %copy-done.48, f32[1024]{0:T(1024)S(1)} %copy-done.37, f32[1024]{0:T(1024)S(1)} %copy-done.32, f32[1024]{0:T(1024)S(1)} %copy-done.26), kind=kOutput, calls=%fused_computation.90 | convolution fusion | flops 8599371776 | bytes 20987904 | tf_op jit(solution)/shard_map/dot_general | solution.py:229
  707.8 12.2 %copy.125 = bf16[128,8,8,512]{3,2,1,0:T(8,128)(2,1)} copy(bf16[128,8,8,512]{3,1,2,0:T(8,128)(2,1)} %bitcast.287) | data formatting | bytes 16777216
  762.4 89.7 %reduce-scatter.11.cloned.1.call-done = bf16[1,512,512]{2,1,0:T(8,128)(2,1)} async-done(((bf16[16,512,512]{2,1,0:T(8,128)(2,1)}), bf16[1,512,512]{2,1,0:T(8,128)(2,1)}) %reduce-scatter.11.cloned.1.call-update) | async-done | bytes 524304 | tf_op jit(solution)/shard_map/reduce_scatter | solution.py:39
  852.1 107.2 %reduce-scatter.9.cloned.1.call-done = bf16[1,512,512]{2,1,0:T(8,128)(2,1)} async-done(((bf16[16,512,512]{2,1,0:T(8,128)(2,1)}), bf16[1,512,512]{2,1,0:T(8,128)(2,1)}) %reduce-scatter.9.cloned.1.call-update) | async-done | bytes 524304 | tf_op jit(solution)/shard_map/reduce_scatter | solution.py:39
  977.7 39.8 %all-gather.20.cloned.1.call-done = f32[393216]{0:T(1024)} async-done(((f32[12288]{0:T(1024)}), f32[393216]{0:T(1024)}) %all-gather.20.cloned.1.call-update) | async-done | bytes 1572880 | tf_op jit(solution)/shard_map/all_gather | solution.py:285
  1021.3 49.2 %all-reduce.3.cloned.1.call-done = (bf16[3,512,128]{2,1,0:T(8,128)(2,1)}, bf16[128,512]{1,0:T(8,128)(2,1)}, bf16[512,512]{1,0:T(8,128)(2,1)}, bf16[512,512]{1,0:T(8,128)(2,1)}) async-done(((bf16[3,512,128]{2,1,0:T(8,128)(2,1)}, bf16[128,512]{1,0:T(8,128)(2,1)}, bf16[512,512]{1,0:T(8,128)(2,1)}, bf16[512,512]{1,0:T(8,128)(2,1)}), (bf16[3,512,128]{2,1,0:T(8,128)(2,1)}, bf16[128,512]{1,0:T(8,128)(2,1)}, ...) | async-done | bytes 1572880 | tf_op jit(solution)/shard_map/psum | solution.py:40
  (323 shorter events, 444.0 us)
Async XLA Ops:
  7.2 36.1 %copy-start = (s32[8,1024]{1,0:T(8,128)S(1)}, s32[8,1024]{1,0:T(8,128)}, u32[]{:S(2)}) copy-start(s32[8,1024]{1,0:T(8,128)} %param.20) | copy-start | bytes 98308
  7.2 33.5 %copy-start.18 = (bf16[1024,1024]{1,0:T(8,128)(2,1)S(1)}, bf16[1024,1024]{1,0:T(8,128)(2,1)}, u32[]{:S(2)}) copy-start(bf16[1024,1024]{1,0:T(8,128)(2,1)} %param.33) | copy-start | bytes 6291460
  7.2 47.2 %all-gather.14.cloned.1.call-start = ((), (), s32[]{:S(2)}) async-start(), calls=%async_computation.9 | async-start | bytes 2228224 | tf_op jit(solution)/shard_map/all_gather | solution.py:18
  8.0 109.0 %all-gather.12.cloned.1.call-start = ((), (), s32[]{:S(2)}) async-start(), calls=%async_computation.8 | async-start | bytes 6684672 | tf_op jit(solution)/shard_map/all_gather | solution.py:18
  8.7 249.9 %all-gather.16.cloned.1.call-start = ((), (), s32[]{:S(2)}) async-start(), calls=%async_computation.10 | async-start | bytes 8912896 | tf_op jit(solution)/shard_map/all_gather | solution.py:18
  9.4 273.3 %all-gather.18.cloned.1.call-start = ((), (), s32[]{:S(2)}) async-start(), calls=%async_computation.11 | async-start | bytes 8912896 | tf_op jit(solution)/shard_map/all_gather | solution.py:18
  10.0 752.4 %reduce-scatter.7.cloned.1.call-start = ((), (), s32[]{:S(2)}) async-start(), calls=%async_computation.5 | async-start | bytes 2228224 | tf_op jit(solution)/shard_map/reduce_scatter | solution.py:39
  165.1 84.4 %copy-start.53 = (f32[1024]{0:T(1024)S(1)}, f32[1024]{0:T(1024)}, u32[]{:S(2)}) copy-start(f32[1024]{0:T(1024)} %param.24) | copy-start | bytes 12292
  309.8 47.7 %copy-start.3 = (f32[1024,1024]{0,1:T(8,128)S(1)}, f32[1024,1024]{0,1:T(8,128)}, u32[]{:S(2)}) copy-start(f32[1024,1024]{0,1:T(8,128)} %copy-done.2) | copy-start | bytes 12582916
  309.8 47.7 %copy-start.14 = (bf16[128,8,8,512]{3,1,2,0:T(8,128)(2,1)S(1)}, bf16[128,8,8,512]{3,1,2,0:T(8,128)(2,1)}, u32[]{:S(2)}) copy-start(bf16[128,8,8,512]{3,1,2,0:T(8,128)(2,1)} %copy.121) | copy-start | bytes 25165828
  309.8 47.7 %copy-start.25 = (f32[1024]{0:T(1024)S(1)}, f32[1024]{0:T(1024)}, u32[]{:S(2)}) copy-start(f32[1024]{0:T(1024)} %copy-done.24) | copy-start | bytes 12292
  309.8 47.7 %copy-start.31 = (f32[1024]{0:T(1024)S(1)}, f32[1024]{0:T(1024)}, u32[]{:S(2)}) copy-start(f32[1024]{0:T(1024)} %copy-done.30) | copy-start | bytes 12292
  309.8 47.7 %copy-start.36 = (f32[1024]{0:T(1024)S(1)}, f32[1024]{0:T(1024)}, u32[]{:S(2)}) copy-start(f32[1024]{0:T(1024)} %param.25) | copy-start | bytes 12292
  309.8 47.7 %copy-start.47 = (f32[1024]{0:T(1024)S(1)}, f32[1024]{0:T(1024)}, u32[]{:S(2)}) copy-start(f32[1024]{0:T(1024)} %param.26) | copy-start | bytes 12292
  309.9 47.7 %copy-start.54 = (f32[1024]{0:T(1024)S(1)}, f32[1024]{0:T(1024)}, u32[]{:S(2)}) copy-start(f32[1024]{0:T(1024)} %param.30) | copy-start | bytes 12292
  369.2 27.9 %copy-start.4 = (f32[1024,1024]{0,1:T(8,128)}, f32[1024,1024]{0,1:T(8,128)S(1)}, u32[]{:S(2)}) copy-start(f32[1024,1024]{0,1:T(8,128)S(1)} %get-tuple-element.281) | copy-start | bytes 12582916
  369.2 27.8 %copy-start.27 = (f32[1024]{0:T(1024)}, f32[1024]{0:T(1024)S(1)}, u32[]{:S(2)}) copy-start(f32[1024]{0:T(1024)S(1)} %broadcast_multiply_fusion.4) | copy-start | bytes 12292
  372.3 24.8 %slice-start = ((s8[8388608]{0:T(1024)(128)(4,1)}), s8[4194304]{0:T(1024)(128)(4,1)S(1)}, s32[]{:S(2)}) async-start(s8[8388608]{0:T(1024)(128)(4,1)} %bitcast.282), calls=%async_computation.14 | async-start | bytes 8388608
  597.0 165.4 %reduce-scatter.5.cloned.1.call-start = ((), (), s32[]{:S(2)}) async-start(), calls=%async_computation.4 | async-start | bytes 6684672 | tf_op jit(solution)/shard_map/reduce_scatter | solution.py:39
  649.7 202.4 %reduce-scatter.11.cloned.1.call-start = ((), (), s32[]{:S(2)}) async-start(), calls=%async_computation.7 | async-start | bytes 8912896 | tf_op jit(solution)/shard_map/reduce_scatter | solution.py:39
  691.6 267.7 %reduce-scatter.9.cloned.1.call-start = ((), (), s32[]{:S(2)}) async-start(), calls=%async_computation.6 | async-start | bytes 8912896 | tf_op jit(solution)/shard_map/reduce_scatter | solution.py:39
  737.2 280.3 %all-gather.20.cloned.1.call-start = ((), (), s32[]{:S(2)}) async-start(), calls=%async_computation.12 | async-start | bytes 1622016 | tf_op jit(solution)/shard_map/all_gather | solution.py:285
  748.5 321.9 %all-reduce.3.cloned.1.call-start = ((), (), s32[]{:S(2)}) async-start(), calls=%async_computation.13 | async-start | bytes 3145728 | tf_op jit(solution)/shard_map/psum | solution.py:40
  975.2 102.2 %copy-start.1 = (s32[8,1024]{1,0:T(8,128)S(1)}, s32[8,1024]{1,0:T(8,128)}, u32[]{:S(2)}) copy-start(s32[8,1024]{1,0:T(8,128)} %param.20) | copy-start | bytes 98308
  (43 other events, 257.5 us)
Sparse Core Ops, SparseCore 0:
  10.2 44.1 all-gather.13
  56.8 60.1 all-gather.11
  119.1 72.9 all-gather.15
  194.2 72.9 all-gather.17
  597.1 60.4 reduce-scatter.6
  661.3 84.0 reduce-scatter.4
  749.5 102.5 reduce-scatter.10
  856.2 103.0 reduce-scatter.8
  962.9 54.6 all-gather.19
  1019.9 50.4 all-reduce.2
where the time goes:
time: 1100 us; the launch traced here: 1080 us
  matrix products  363 us (33%)
  waiting for transfers between devices  358 us (33%)
  local copies, waits for them, and re-layouts  222 us (20%)
  other arithmetic  98.6 us (9%)
  blocking collectives  26.5 us (2%)
  between operations  15.4 us (1%)
    reduce_scatter x4, waiting for transfers between devices, scatter_blocks(): owned = lax.psum_scatter(flat, OWNERS, scatter_dimension=0, tiled=False)  197 us
    all_gather x4, waiting for transfers between devices, gather_blocks(): blocks = lax.all_gather(weight, OWNERS, axis=0, tiled=False)  69.3 us
    unnamed x132, local copies, waits for them, and re-layouts  66.8 us
    psum x1, waiting for transfers between devices, scatter_blocks(): return lax.psum(owned, 'replica').astype(jnp.float32)  49.2 us
    dot_general x1, matrix products, body(): jnp.dot(hidden_low, w_up, preferred_element_type=jnp.float32) + bias_up  47.6 us
    reshape x4, local copies, waits for them, and re-layouts, gather_blocks(): blocks.reshape((lax.axis_size('shard'), lax.axis_size('tensor')) + weight...  46.9 us
    dot_general x16, matrix products, masked_scores(): jnp.einsum('qhd,khd->hqk', queries, key_rows, preferred_element_type=jnp....  41.3 us
    all_gather x1, waiting for transfers between devices, body(): lax.all_gather(jnp.concatenate(parts), EVERYONE, axis=0, tiled=False)  39.8 us
  transfers between devices with their start and end apart: 10, of which 6 were waited for; matrix products, arithmetic and copies ran while one was open for 33% of the time, Pallas kernels for 0%

commit v1 on v0

--- a/solution.py
+++ b/solution.py
@@ -37,7 +37,7 @@
 def scatter_blocks(blocks):
     flat = blocks.reshape((-1,) + blocks.shape[2:])
     owned = lax.psum_scatter(flat, OWNERS, scatter_dimension=0, tiled=False)
-    return lax.psum(owned, "replica").astype(jnp.float32)
+    return jnp.sum(lax.all_gather(owned, "replica"), axis=0).astype(jnp.float32)
 
 
 def scatter_qkv(grad):

time: 1100 us -> 941 us (0.86)
  waiting for transfers between devices: 358 us -> 187 us
  blocking collectives: 26.5 us -> 46.4 us
  matrix products: 363 us -> 375 us
    reduce_scatter x4, waiting for transfers between devices: 197 us -> 87.6 us  [scatter_blocks(): owned = lax.psum_scatter(flat, OWNERS, scatter_dimension=0, tiled=False)]
    psum x1 -> x0, waiting for transfers between devices: 49.2 us -> none  [scatter_blocks(): return lax.psum(owned, 'replica').astype(jnp.float32)]
    transpose x5 -> x0, local copies, waits for them, and re-layouts: 45.3 us -> none  [the longest x2 17.1 us: scatter_row_col(): return scatter_blocks(blocks.transpose(0, 2, 1, 3))]
    all_gather x1, waiting for transfers between devices: 39.8 us -> 0.01 us  [body(): lax.all_gather(jnp.concatenate(parts), EVERYONE, axis=0, tiled=False)]
    all_gather x0 -> x2, waiting for transfers between devices: none -> 26.9 us  [scatter_blocks(): return jnp.sum(lax.all_gather(owned, 'replica'), axis=0).astype(jnp.float32)]
    all_gather x0 -> x2, blocking collectives: none -> 19.9 us  [scatter_blocks(): return jnp.sum(lax.all_gather(owned, 'replica'), axis=0).astype(jnp.float32)]
    another operation x3 -> x6, local copies, waits for them, and re-layouts: 12.4 us -> 28.5 us  [body(): jnp.stack([lax.dot_general(layer_input, grad, CONTRACT_ROWS, preferred_el...]
    transpose x1 -> x0, other arithmetic: 12.8 us -> none  [scatter_qkv(): return scatter_blocks(blocks.transpose(1, 3, 0, 2, 4))]
  transfers between devices with their start and end apart: 10 -> 11, of which waited for: 6 -> 6; matrix products, arithmetic and copies ran while one was open for 33% -> 58% of each run, Pallas kernels for 0% -> 0%
where the time goes in v1:
time: 941 us; the launch traced here: 927 us
  matrix products  375 us (40%)
  local copies, waits for them, and re-layouts  213 us (23%)
  waiting for transfers between devices  187 us (20%)
  other arithmetic  90.1 us (10%)
  blocking collectives  46.4 us (5%)
  between operations  15 us (2%)
    reduce_scatter x4, waiting for transfers between devices, scatter_blocks(): owned = lax.psum_scatter(flat, OWNERS, scatter_dimension=0, tiled=False)  87.6 us
    unnamed x94, local copies, waits for them, and re-layouts  70.1 us
    all_gather x4, waiting for transfers between devices, gather_blocks(): blocks = lax.all_gather(weight, OWNERS, axis=0, tiled=False)  69.5 us
    dot_general x1, matrix products, body(): jnp.dot(hidden_low, w_up, preferred_element_type=jnp.float32) + bias_up  47.8 us
    reshape x4, local copies, waits for them, and re-layouts, gather_blocks(): blocks.reshape((lax.axis_size('shard'), lax.axis_size('tensor')) + weight...  46.8 us
    dot_general x16, matrix products, masked_scores(): jnp.einsum('qhd,khd->hqk', queries, key_rows, preferred_element_type=jnp....  41.4 us
    dot_general x8, matrix products, attend(): jnp.einsum('hqk,khd->qhd', attn_probs.astype(jnp.bfloat16), value_rows, p...  35.2 us
    dot_general x8, matrix products, attend_back(): jnp.einsum('hqk,qhd->khd', attn_probs.astype(jnp.bfloat16), mixed_grad, p...  34.2 us
  transfers between devices with their start and end apart: 11, of which 6 were waited for; matrix products, arithmetic and copies ran while one was open for 58% of the time, Pallas kernels for 0%

profile of v1, /device:TPU:0, one launch (start us, length us, event | category | flops | bytes accessed | tf_op | source)
XLA Modules:
  0.0 927.4 jit_solution(11224028913519090012)
XLA Ops:
  10.1 13.7 %all_gather.50 = f32[2,1024]{1,0:T(2,128)S(1)} all-gather(f32[2,128]{1,0:T(2,128)} %param.22), channel_id=1, replica_groups=mesh['replica'=2,'shard'=2,'tensor'=8] {'tensor'}, dimensions={1}, use_global_device_ids=true | all-gather | bytes 9216 | tf_op jit(solution)/shard_map/all_gather | solution.py:152
  28.0 12.8 %all-gather.5 = f32[8,1,512]{2,1,0:T(1,128)S(1)} all-gather(f32[1,1,512]{2,1,0:T(1,128)S(1)} %bitcast.300), channel_id=1, replica_groups=mesh['replica'=2,'shard'=2,'tensor'=8] {'tensor'}, dimensions={0}, use_global_device_ids=true | all-gather | bytes 18432 | tf_op jit(solution)/shard_map/all_gather | solution.py:153
  43.3 11.3 %all-gather.20.cloned.1.call-done = bf16[2048,512]{1,0:T(8,128)(2,1)} async-done(((bf16[128,512]{1,0:T(8,128)(2,1)}), bf16[2048,512]{1,0:T(8,128)(2,1)}) %all-gather.20.cloned.1.call-update) | async-done | bytes 2097168 | tf_op jit(solution)/shard_map/all_gather | solution.py:18
  58.8 58.2 %all-gather.18.cloned.1.call-done = bf16[48,512,128]{2,1,0:T(8,128)(2,1)} async-done(((bf16[3,512,128]{2,1,0:T(8,128)(2,1)}), bf16[48,512,128]{2,1,0:T(8,128)(2,1)}) %all-gather.18.cloned.1.call-update) | async-done | bytes 6291472 | tf_op jit(solution)/shard_map/all_gather | solution.py:18
  117.0 16.2 %copy.94 = bf16[2,8,3,512,128]{3,0,4,1,2:T(2,128)(2,1)} copy(bf16[2,8,3,512,128]{4,3,2,1,0:T(8,128)(2,1)} %bitcast.286) | data formatting | bytes 12582912 | tf_op jit(solution)/shard_map/reshape | solution.py:19
  133.2 11.0 %reshape.287 = bf16[3,1024,1024]{1,2,0:T(8,128)(2,1)} reshape(bf16[3,2,512,8,128]{2,1,4,3,0:T(2,128)(2,1)} %bitcast.261) | data formatting | bytes 12582912 | tf_op jit(solution)/shard_map/reshape | solution.py:24
  165.2 84.3 %while.28 = (s32[]{:T(128)}, bf16[8,1024,2,64]{1,3,2,0:T(8,128)(2,1)}, f32[8,2,1024,1]{2,1,3,0:T(2,128)}, bf16[8,1024,2,64]{1,3,2,0:T(8,128)(2,1)}, bf16[8,1024,...) while((s32[]{:T(128)}, ...), condition=%wide.region_3.4_spmd.clone, body=%wide.region_0.3_spmd.clone.sunk | while | flops 563214336 | bytes 30480980 | solution.py:193
  258.7 11.5 %copy.96 = bf16[2,8,512,512]{3,1,2,0:T(8,128)(2,1)} copy(bf16[2,8,512,512]{3,2,1,0:T(8,128)(2,1)} %bitcast.274) | data formatting | bytes 16777216 | tf_op jit(solution)/shard_map/reshape | solution.py:19
  270.2 12.4 %copy.122 = bf16[128,8,8,512]{3,1,2,0:T(8,128)(2,1)} copy(bf16[128,8,8,512]{3,2,1,0:T(8,128)(2,1)} %bitcast.265) | data formatting | bytes 16777216
  282.6 14.9 %copy.97 = bf16[2,8,512,512]{2,1,3,0:T(8,128)(2,1)} copy(bf16[2,8,512,512]{3,2,1,0:T(8,128)(2,1)} %bitcast.275) | data formatting | bytes 16777216 | tf_op jit(solution)/shard_map/reshape | solution.py:19
  297.5 12.2 %copy.123 = bf16[128,8,8,512]{3,1,2,0:T(8,128)(2,1)} copy(bf16[128,8,8,512]{3,2,1,0:T(8,128)(2,1)} %bitcast.266) | data formatting | bytes 16777216
  309.7 47.8 %fusion.60 = (bf16[1024,4096]{1,0:T(8,128)(2,1)}, f32[1024,4096]{1,0:T(8,128)}) fusion(f32[4096]{0:T(1024)S(1)} %bitcast.298, bf16[1024,4096]{1,0:T(8,128)(2,1)} %bitcast.276, bf16[1024,1024]{0,1:T(8,128)(2,1)S(1)} %fusion.108.clone.4), kind=kOutput, calls=%fused_computation.67 | convolution fusion | flops 8866758656 | bytes 35667968 | tf_op jit(solution)/shard_map/dot_general | solution.py:206
  357.6 11.7 %fusion.117 = (f32[1024]{0:T(1024)S(1)}, f32[1024,1024]{0,1:T(8,128)S(1)}) fusion(f32[1024]{0:T(1024)S(1)} %copy-done.35, bf16[1024,4096]{1,0:T(8,128)(2,1)} %get-tuple-element.274, bf16[4096,1024]{0,1:T(8,128)(2,1)S(1)} %bitcast.279, f32[1024]{0:T(1024)S(1)} %copy-done.30, f32[1024]{0:T(1024)S(1)} %copy-done.26, f32[1024]{0:T(1024)S(1)} %copy-done.24, ...), kind=kOutput, calls=%fused_computation.175 | convolution fusion | flops 8597273600 | bytes 25190400 | tf_op jit(solution)/shard_map/dot_general | solution.py:209
  374.8 12.9 %convolution_convert_fusion = bf16[4096,1024]{1,0:T(8,128)(2,1)} fusion(bf16[1024,4096]{1,0:T(8,128)(2,1)S(1)} %copy-done.36, bf16[1024,1024]{0,1:T(8,128)(2,1)S(1)} %copy-done.7, f32[1024,1024]{0,1:T(8,128)S(1)} %get-tuple-element.277, f32[1024]{0:T(1024)S(1)} %broadcast_multiply_fusion.2, f32[1024]{0:T(1024)S(1)} %broadcast_multiply_fusion.3, ...), kind=kOutput, calls=%fused_computation.88 | convolution fusion | flops 8603566080 | bytes 23089152 | tf_op jit(solution)/shard_map/dot_general | solution.py:217
  387.7 14.5 %reshape.301 = bf16[8,512,2,512]{3,2,1,0:T(2,128)(2,1)} reshape(bf16[4096,1024]{1,0:T(8,128)(2,1)} %convolution_convert_fusion) | data formatting | bytes 16777216 | tf_op jit(solution)/shard_map/reshape | solution.py:60
  410.6 22.8 %fusion.118 = (f32[4096]{0:T(1024)}, bf16[1024,4096]{1,0:T(8,128)(2,1)S(1)}) fusion(f32[1024,4096]{1,0:T(8,128)} %get-tuple-element.275, f32[4096]{0:T(1024)S(1)} %bitcast.299, bf16[4096,1024]{0,1:T(8,128)(2,1)} %bitcast.278, f32[1024]{0:T(1024)S(1)} %broadcast_multiply_fusion.2, f32[1024,1024]{0,1:T(8,128)} %copy-done.5, ...), kind=kOutput, calls=%fused_computation.176 | convolution fusion | flops 8649699328 | bytes 39899136 | tf_op jit(solution)/shard_map/dot_general | solution.py:221
  433.3 11.9 %convolution_convert_fusion.1 = bf16[1024,4096]{1,0:T(8,128)(2,1)} fusion(bf16[1024,4096]{1,0:T(8,128)(2,1)S(1)} %get-tuple-element.280, f32[1024,1024]{0,1:T(8,128)S(1)} %copy-done.4, f32[1024]{0:T(1024)S(1)} %copy-done.30, f32[1024]{0:T(1024)S(1)} %copy-done.26, f32[1024]{0:T(1024)S(1)} %copy-done.24, f32[1024]{0:T(1024)S(1)} %copy-done.21), kind=kOutput, calls=%fused_computation.89 | convolution fusion | flops 8599371776 | bytes 20987904 | tf_op jit(solution)/shard_map/dot_general | solution.py:229
  445.3 12.2 %copy.127 = bf16[128,8,8,512]{3,2,1,0:T(8,128)(2,1)} copy(bf16[128,8,8,512]{3,1,2,0:T(8,128)(2,1)} %bitcast.280) | data formatting | bytes 16777216
  467.1 17.2 %multiply_reduce_fusion.1 = (f32[1024]{0:T(1024)S(1)}, f32[1024]{0:T(1024)S(1)}, f32[1024]{0:T(1024)S(1)}, f32[1024]{0:T(1024)S(1)}, f32[1024,1024]{0,1:T(8,128)S(1)}) fusion(f32[1024,1024]{0,1:T(8,128)S(1)} %copy-done.4, f32[1024]{0:T(1024)S(1)} %copy-done.24, f32[1024]{0:T(1024)S(1)} %copy-done.21, f32[1024]{0:T(1024)S(1)} %copy-done.26, ...), kind=kOutput, calls=%fused_computation.107 | convolution fusion | flops 8608804864 | bytes 31506432 | tf_op jit(solution)/shard_map/dot_general | solution.py:233
  490.5 164.5 %while.29 = (s32[]{:T(128)}, f32[8,1024,2,64]{1,3,2,0:T(8,128)}, bf16[8,1024,2,64]{1,3,2,0:T(8,128)(2,1)}, f32[8,1024,2,64]{1,3,2,0:T(8,128)}, bf16[8,1024,2,64]...) while((s32[]{:T(128)}, f32[8,1024,2,64]{1,3,2,0:T(8,128)}, ...), condition=%wide.region_14.15_spmd.clone, body=%wide.region_12.14_spmd.clone.sunk | while | flops 1374943232 | bytes 70583408 | solution.py:249
  756.7 10.0 %add_add_fusion = f32[1024,1024]{0,1:T(8,128)} fusion(f32[1024,1024]{0,1:T(8,128)} %fusion.120, f32[1024,1024]{0,1:T(8,128)} %copy-done.6, f32[1024,1024]{0,1:T(8,128)} %fusion.119, bf16[1024,1024]{0,1:T(8,128)(2,1)S(1)} %bitcast.272, bf16[1024,1024]{0,1:T(8,128)(2,1)} %bitcast.285), kind=kOutput, calls=%fused_computation.108 | convolution fusion | flops 2150629376 | bytes 20971520 | tf_op jit(solution)/shard_map/dot_general | solution.py:271
  791.3 81.4 %reduce-scatter.5.cloned.1.call-done = bf16[1,3,512,128]{3,2,1,0:T(8,128)(2,1)} async-done(((bf16[16,3,512,128]{3,2,1,0:T(8,128)(2,1)}), bf16[1,3,512,128]{3,2,1,0:T(8,128)(2,1)}) %reduce-scatter.5.cloned.1.call-update) | async-done | bytes 393232 | tf_op jit(solution)/shard_map/reduce_scatter | solution.py:39
  872.7 14.1 %all_gather.58 = bf16[2,3,512,128]{3,2,1,0:T(8,128)(2,1)S(1)} all-gather(bf16[1,3,512,128]{3,2,1,0:T(8,128)(2,1)} %reduce-scatter.5.cloned.1.call-done), channel_id=1, replica_groups=mesh['replica'=2,'shard'=2,'tensor'=8] {'replica'}, dimensions={0}, use_global_device_ids=true | all-gather | bytes 1179648 | tf_op jit(solution)/shard_map/all_gather | solution.py:40
  898.0 19.7 %all-gather.14.cloned.1.call-done = bf16[2,512,512]{2,1,0:T(8,128)(2,1)} async-done(((bf16[1,512,512]{2,1,0:T(8,128)(2,1)}), bf16[2,512,512]{2,1,0:T(8,128)(2,1)}) %all-gather.14.cloned.1.call-update) | async-done | bytes 1048592 | tf_op jit(solution)/shard_map/all_gather | solution.py:40
  (294 shorter events, 461.8 us)
Async XLA Ops:
  7.2 36.1 %copy-start = (s32[8,1024]{1,0:T(8,128)S(1)}, s32[8,1024]{1,0:T(8,128)}, u32[]{:S(2)}) copy-start(s32[8,1024]{1,0:T(8,128)} %param.20) | copy-start | bytes 98308
  7.2 20.8 %copy-start.32 = (f32[512]{0:T(512)S(1)}, f32[512]{0:T(512)}, u32[]{:S(2)}) copy-start(f32[512]{0:T(512)} %param.28) | copy-start | bytes 6148
  7.2 33.5 %copy-start.13 = (bf16[1024,1024]{1,0:T(8,128)(2,1)S(1)}, bf16[1024,1024]{1,0:T(8,128)(2,1)}, u32[]{:S(2)}) copy-start(bf16[1024,1024]{1,0:T(8,128)(2,1)} %param.33) | copy-start | bytes 6291460
  7.2 47.3 %all-gather.20.cloned.1.call-start = ((), (), s32[]{:S(2)}) async-start(), calls=%async_computation.11 | async-start | bytes 2228224 | tf_op jit(solution)/shard_map/all_gather | solution.py:18
  8.0 109.1 %all-gather.18.cloned.1.call-start = ((), (), s32[]{:S(2)}) async-start(), calls=%async_computation.10 | async-start | bytes 6684672 | tf_op jit(solution)/shard_map/all_gather | solution.py:18
  8.7 250.0 %all-gather.22.cloned.1.call-start = ((), (), s32[]{:S(2)}) async-start(), calls=%async_computation.12 | async-start | bytes 8912896 | tf_op jit(solution)/shard_map/all_gather | solution.py:18
  9.4 273.1 %all-gather.24.cloned.1.call-start = ((), (), s32[]{:S(2)}) async-start(), calls=%async_computation.13 | async-start | bytes 8912896 | tf_op jit(solution)/shard_map/all_gather | solution.py:18
  10.0 735.4 %reduce-scatter.11.cloned.1.call-start = ((), (), s32[]{:S(2)}) async-start(), calls=%async_computation.8 | async-start | bytes 8912896 | tf_op jit(solution)/shard_map/reduce_scatter | solution.py:39
  165.2 84.4 %copy-start.34 = (f32[1024]{0:T(1024)S(1)}, f32[1024]{0:T(1024)}, u32[]{:S(2)}) copy-start(f32[1024]{0:T(1024)} %param.24) | copy-start | bytes 12292
  309.6 47.9 %copy-start.3 = (f32[1024,1024]{0,1:T(8,128)S(1)}, f32[1024,1024]{0,1:T(8,128)}, u32[]{:S(2)}) copy-start(f32[1024,1024]{0,1:T(8,128)} %copy-done.2) | copy-start | bytes 12582916
  309.6 47.9 %copy-start.10 = (bf16[128,8,8,512]{3,1,2,0:T(8,128)(2,1)S(1)}, bf16[128,8,8,512]{3,1,2,0:T(8,128)(2,1)}, u32[]{:S(2)}) copy-start(bf16[128,8,8,512]{3,1,2,0:T(8,128)(2,1)} %copy.123) | copy-start | bytes 25165828
  309.6 47.9 %copy-start.21 = (f32[1024]{0:T(1024)S(1)}, f32[1024]{0:T(1024)}, u32[]{:S(2)}) copy-start(f32[1024]{0:T(1024)} %copy-done.20) | copy-start | bytes 12292
  309.6 47.9 %copy-start.24 = (f32[1024]{0:T(1024)S(1)}, f32[1024]{0:T(1024)}, u32[]{:S(2)}) copy-start(f32[1024]{0:T(1024)} %copy-done.23) | copy-start | bytes 12292
  309.6 47.9 %copy-start.26 = (f32[1024]{0:T(1024)S(1)}, f32[1024]{0:T(1024)}, u32[]{:S(2)}) copy-start(f32[1024]{0:T(1024)} %param.25) | copy-start | bytes 12292
  309.7 47.9 %copy-start.30 = (f32[1024]{0:T(1024)S(1)}, f32[1024]{0:T(1024)}, u32[]{:S(2)}) copy-start(f32[1024]{0:T(1024)} %param.26) | copy-start | bytes 12292
  309.7 47.9 %copy-start.35 = (f32[1024]{0:T(1024)S(1)}, f32[1024]{0:T(1024)}, u32[]{:S(2)}) copy-start(f32[1024]{0:T(1024)} %param.30) | copy-start | bytes 12292
  410.5 346.2 %reduce-scatter.9.cloned.1.call-start = ((), (), s32[]{:S(2)}) async-start(), calls=%async_computation.6 | async-start | bytes 8912896 | tf_op jit(solution)/shard_map/reduce_scatter | solution.py:39
  410.5 22.8 %copy-start.4 = (f32[1024,1024]{0,1:T(8,128)S(1)}, f32[1024,1024]{0,1:T(8,128)}, u32[]{:S(2)}) copy-start(f32[1024,1024]{0,1:T(8,128)} %copy-done.2) | copy-start | bytes 12582916
  489.8 284.9 %all-gather.26.cloned.1.call-start = ((), (), s32[]{:S(2)}) async-start(), calls=%async_computation.14 | async-start | bytes 1622016 | tf_op jit(solution)/shard_map/all_gather | solution.py:285
  666.1 118.5 %reduce-scatter.7.cloned.1.call-start = ((), (), s32[]{:S(2)}) async-start(), calls=%async_computation.5 | async-start | bytes 2228224 | tf_op jit(solution)/shard_map/reduce_scatter | solution.py:39
  678.0 194.6 %reduce-scatter.5.cloned.1.call-start = ((), (), s32[]{:S(2)}) async-start(), calls=%async_computation.4 | async-start | bytes 6684672 | tf_op jit(solution)/shard_map/reduce_scatter | solution.py:39
  733.2 162.1 %all-gather.16.cloned.1.call-start = ((), (), s32[]{:S(2)}) async-start(), calls=%async_computation.9 | async-start | bytes 1572864 | tf_op jit(solution)/shard_map/all_gather | solution.py:40
  745.4 172.3 %all-gather.14.cloned.1.call-start = ((), (), s32[]{:S(2)}) async-start(), calls=%async_computation.7 | async-start | bytes 1572864 | tf_op jit(solution)/shard_map/all_gather | solution.py:40
  872.7 47.8 %copy-start.1 = (s32[8,1024]{1,0:T(8,128)S(1)}, s32[8,1024]{1,0:T(8,128)}, u32[]{:S(2)}) copy-start(s32[8,1024]{1,0:T(8,128)} %param.20) | copy-start | bytes 98308
  (25 other events, 110.5 us)
Sparse Core Ops, SparseCore 0:
  10.2 44.2 all-gather.19
  56.9 60.1 all-gather.17
  119.2 73.0 all-gather.21
  194.4 72.8 all-gather.23
  410.6 102.0 reduce-scatter.10
  516.6 103.1 reduce-scatter.8
  666.3 53.8 all-gather.25
  723.9 60.7 reduce-scatter.6
  788.6 84.0 reduce-scatter.4
  874.1 21.1 all-gather.15
  896.8 20.8 all-gather.13
